TPU v7x, 32 devices: a whole 2x2x4 slice. The times are simulated.
32 devices in a mesh: section: 2 (over x), expert: 4 (over y, core), dp: 4 (over z).
Axes of the slice: x: 2, y: 2, z: 4, core: 2. Of those that a mesh axis runs over, the one named last changes fastest.
Arguments:
- inputs: bfloat16 [4, 512, 3072], P(None, ('expert', 'dp')), may hold values from -6 to 6
- upstream: bfloat16 [4, 512, 3072], P(None, ('expert', 'dp')), may hold values from -1.5 to 1.5
- route_mask: int32 [2, 4, 512], P('section', None, ('expert', 'dp')), may hold values from 0 to 1, as said below
- route_weights: float32 [2, 4, 512], P('section', None, ('expert', 'dp')), may hold values from 0.2 to 1
- gate_weight: bfloat16 [2, 3072, 8192], P('section', None, ('expert', 'dp')), may hold values from -0.109375 to 0.109375
- up_weight: bfloat16 [2, 3072, 8192], P('section', None, ('expert', 'dp')), may hold values from -0.109375 to 0.109375
- down_weight: bfloat16 [2, 8192, 3072], P('section', ('expert', 'dp')), may hold values from -0.0625 to 0.0625
Outputs:
- gate_grad: bfloat16 [2, 3072, 8192], P('section', None, ('expert', 'dp'))
- up_grad: bfloat16 [2, 3072, 8192], P('section', None, ('expert', 'dp'))
- down_grad: bfloat16 [2, 8192, 3072], P('section', ('expert', 'dp'))
Inputs may be any that keep to these rules, and one draw needn't show every extreme that they name: `route_mask`: in each layer and micro-batch, each aligned block of 32 tokens (the tokens of one device) has at most 8 ones, and some block exactly 8.
All inputs are finite; a program needn't handle non-finite values.
Results may differ from a plain program's by a relative error of at most 0.0095.
Values may be sent and summed in bfloat16 or wider, within the bound.
A program may use at most 128 MiB of HBM per device.

v0:
```python
import jax
import jax.numpy as jnp
from jax import lax
from jax.sharding import PartitionSpec as P

CAP = 8
EPSILON = 1e-05


def shifted(block, axis, distance):
    devices = range(lax.axis_size(axis))
    route = [(i - distance, i) for i in devices if i - distance in devices]
    return lax.ppermute(block, axis, route)


def normalize(layer_input):
    input_f = layer_input.astype(jnp.float32)
    scale = lax.rsqrt(jnp.mean(input_f * input_f, axis=-1, keepdims=True) + EPSILON)
    return (input_f, scale, (input_f * scale).astype(jnp.bfloat16))


def slot_table(mask_row):
    position = jnp.cumsum(mask_row) - 1
    chosen = (mask_row[:, None] == 1) & (
        position[:, None] == jnp.arange(CAP, dtype=jnp.int32)[None, :]
    )
    return chosen.astype(jnp.bfloat16)


def pick_rows(table, values):
    return lax.dot_general(
        table, values, (((0,), (0,)), ((), ())), preferred_element_type=jnp.float32
    ).astype(jnp.bfloat16)


def layer_forward(layer_input, mask_row, weight_row, gate_w, up_w, down_w):
    input_f, scale, normed = normalize(layer_input)
    table = slot_table(mask_row)
    send_rows = pick_rows(table, normed)
    rows = lax.all_gather(send_rows, ("expert", "dp"), axis=0, tiled=True)
    gate_pre = jnp.dot(rows, gate_w, preferred_element_type=jnp.float32)
    up_pre = jnp.dot(rows, up_w, preferred_element_type=jnp.float32)
    hidden = (jax.nn.silu(gate_pre) * up_pre).astype(jnp.bfloat16)
    summed = lax.psum_scatter(
        jnp.dot(hidden, down_w, preferred_element_type=jnp.float32).astype(jnp.bfloat16),
        ("expert", "dp"),
        scatter_dimension=0,
        tiled=True,
    )
    back = jnp.dot(table, summed, preferred_element_type=jnp.float32)
    output = (input_f + weight_row[:, None] * back).astype(jnp.bfloat16)
    return (output, rows)


def layer_backward(layer_input, mask_row, weight_row, gate_w, up_w, down_w, flowing):
    contract_rows = (((1,), (1,)), ((), ()))
    input_f, scale, normed = normalize(layer_input)
    table = slot_table(mask_row)
    flowing_f = flowing.astype(jnp.float32)
    out_grad = (weight_row[:, None] * flowing_f).astype(jnp.bfloat16)
    send_grad = pick_rows(table, out_grad)
    send_rows = pick_rows(table, normed)
    rows, grad_rows = (
        lax.all_gather(send_rows, ("expert", "dp"), axis=0, tiled=True),
        lax.all_gather(send_grad, ("expert", "dp"), axis=0, tiled=True),
    )
    gate_pre = jnp.dot(rows, gate_w, preferred_element_type=jnp.float32)
    up_pre = jnp.dot(rows, up_w, preferred_element_type=jnp.float32)
    sigma = jax.nn.sigmoid(gate_pre)
    silu_val = jax.nn.silu(gate_pre)
    hidden = (silu_val * up_pre).astype(jnp.bfloat16)
    hidden_grad = lax.dot_general(
        grad_rows, down_w, contract_rows, preferred_element_type=jnp.float32
    )
    gate_pre_grad = (hidden_grad * up_pre * sigma * (1.0 + gate_pre * (1.0 - sigma))).astype(
        jnp.bfloat16
    )
    up_pre_grad = (hidden_grad * silu_val).astype(jnp.bfloat16)
    summed = lax.psum_scatter(
        (
            lax.dot_general(
                gate_pre_grad, gate_w, contract_rows, preferred_element_type=jnp.float32
            )
            + lax.dot_general(up_pre_grad, up_w, contract_rows, preferred_element_type=jnp.float32)
        ).astype(jnp.bfloat16),
        ("expert", "dp"),
        scatter_dimension=0,
        tiled=True,
    )
    total = jnp.dot(table, summed, preferred_element_type=jnp.float32)
    inner = jnp.mean(input_f * total, axis=-1, keepdims=True)
    input_grad = (flowing_f + scale * total - input_f * (scale * scale * scale) * inner).astype(
        jnp.bfloat16
    )
    units = jnp.stack([hidden, gate_pre_grad, up_pre_grad])
    return (input_grad, rows, grad_rows, units)


def store_if(store, index, value, valid):
    older = lax.dynamic_index_in_dim(store, index, 0, keepdims=False)
    return store.at[index].set(jnp.where(valid, value, older))


def shards(inputs, upstream, route_mask, route_weights, gate_weight, up_weight, down_weight):
    sections = lax.axis_size("section")
    section = lax.axis_index("section")
    micro_count = inputs.shape[0]
    token_count = inputs.shape[1]
    model_width = inputs.shape[2]
    hidden_width = gate_weight.shape[2]
    group_rows = lax.axis_size(("expert", "dp")) * CAP
    ticks = micro_count + sections - 1
    gate_w = gate_weight[0]
    up_w = up_weight[0]
    down_w = down_weight[0]
    masks = route_mask[0]
    weights = route_weights[0]
    stash_inputs = jnp.zeros((micro_count, token_count, model_width), jnp.bfloat16)
    stash_rows = jnp.zeros((1,), jnp.bfloat16)

    def forward_tick(tick, carry):
        incoming, stash_inputs, stash_rows = carry
        micro_index = tick - section
        valid = (micro_index >= 0) & (micro_index < micro_count)
        clipped = jnp.clip(micro_index, 0, micro_count - 1)
        first_input = lax.dynamic_index_in_dim(inputs, clipped, 0, keepdims=False)
        current = jnp.where(section == 0, first_input, incoming)
        mask_row = lax.dynamic_index_in_dim(masks, clipped, 0, keepdims=False)
        weight_row = lax.dynamic_index_in_dim(weights, clipped, 0, keepdims=False)
        stash_inputs = store_if(stash_inputs, clipped, current, valid)
        output, rows = layer_forward(current, mask_row, weight_row, gate_w, up_w, down_w)
        finished = jnp.where(valid, output, jnp.zeros_like(output))
        incoming = shifted(finished, "section", 1)
        return (incoming, stash_inputs, stash_rows)

    start = jnp.zeros((token_count, model_width), jnp.bfloat16)
    unused, stash_inputs, stash_rows = lax.fori_loop(
        0, ticks, forward_tick, (start, stash_inputs, stash_rows)
    )
    rows_store = jnp.zeros((micro_count, group_rows, model_width), jnp.bfloat16)
    grads_store = jnp.zeros((micro_count, group_rows, model_width), jnp.bfloat16)
    units_store = jnp.zeros((micro_count, 3, group_rows, hidden_width), jnp.bfloat16)

    def backward_tick(tick, carry):
        incoming, rows_store, grads_store, units_store = carry
        micro_index = tick - (sections - 1 - section)
        valid = (micro_index >= 0) & (micro_index < micro_count)
        clipped = jnp.clip(micro_index, 0, micro_count - 1)
        last_grad = lax.dynamic_index_in_dim(upstream, clipped, 0, keepdims=False)
        current = jnp.where(section == sections - 1, last_grad, incoming)
        mask_row = lax.dynamic_index_in_dim(masks, clipped, 0, keepdims=False)
        weight_row = lax.dynamic_index_in_dim(weights, clipped, 0, keepdims=False)
        layer_input = lax.dynamic_index_in_dim(stash_inputs, clipped, 0, keepdims=False)
        input_grad, rows, grad_rows, units = layer_backward(
            layer_input, mask_row, weight_row, gate_w, up_w, down_w, current
        )
        rows_store = store_if(rows_store, clipped, rows, valid)
        grads_store = store_if(grads_store, clipped, grad_rows, valid)
        units_store = store_if(units_store, clipped, units, valid)
        finished = jnp.where(valid, input_grad, jnp.zeros_like(input_grad))
        incoming = shifted(finished, "section", -1)
        return (incoming, rows_store, grads_store, units_store)

    unused, rows_store, grads_store, units_store = lax.fori_loop(
        0, ticks, backward_tick, (start, rows_store, grads_store, units_store)
    )
    all_rows = rows_store.reshape(-1, model_width)
    all_grads = grads_store.reshape(-1, model_width)
    hidden_all = units_store[:, 0].reshape(-1, hidden_width)
    gate_all = units_store[:, 1].reshape(-1, hidden_width)
    up_all = units_store[:, 2].reshape(-1, hidden_width)
    contract_first = (((0,), (0,)), ((), ()))
    gate_grad = lax.dot_general(
        all_rows, gate_all, contract_first, preferred_element_type=jnp.float32
    )
    up_grad = lax.dot_general(all_rows, up_all, contract_first, preferred_element_type=jnp.float32)
    down_grad = lax.dot_general(
        hidden_all, all_grads, contract_first, preferred_element_type=jnp.float32
    )
    return (
        gate_grad.astype(jnp.bfloat16)[None],
        up_grad.astype(jnp.bfloat16)[None],
        down_grad.astype(jnp.bfloat16)[None],
    )


def solution(mesh):
    return jax.shard_map(
        shards,
        mesh=mesh,
        in_specs=(
            P(None, ("expert", "dp"), None),
            P(None, ("expert", "dp"), None),
            P("section", None, ("expert", "dp")),
            P("section", None, ("expert", "dp")),
            P("section", None, ("expert", "dp")),
            P("section", None, ("expert", "dp")),
            P("section", ("expert", "dp"), None),
        ),
        out_specs=(
            P("section", None, ("expert", "dp")),
            P("section", None, ("expert", "dp")),
            P("section", ("expert", "dp"), None),
        ),
        check_vma=False,
    )
```

profile of v0, /device:TPU:0, one launch (start us, length us, event | category | flops | bytes accessed | tf_op | source)
XLA Modules:
  0.0 1395.9 jit_solution(2319598621400494459)
XLA Ops:
  8.2 588.0 %while.42 = (s32[]{:T(128)}, bf16[32,3072]{1,0:T(8,128)(2,1)S(1)}, bf16[4,32,3072]{2,1,0:T(8,128)(2,1)}, s32[]{:T(128)}, pred[]{:T(512)}, /*index=5*/bf16[4,32,3...) while((s32[]{:T(128)}, bf16[32,3072]{1,0:T(8,128)(2,1)S(1)}, ...), condition=%wide.region_5.6_spmd, body=%wide.region_0.5_spmd.sunk | while | flops 1213294720 | bytes 35229956 | solution.py:137
  12.1 2.6 fusion.143
  15.2 41.6 %all_gather.33 = bf16[128,3072]{1,0:T(8,128)(2,1)S(1)} all-gather(bf16[8,3072]{1,0:T(8,128)(2,1)S(1)} %convolution_convert_fusion.11), channel_id=1, replica_groups=mesh['section'=2,'expert'=4,'dp'=4] {'expert','dp'}, dimensions={0}, use_global_device_ids=true | all-gather | bytes 835584 | tf_op jit(solution)/shard_map/while/body/eval_jaxpr/all_gather | solution.py:40
  57.7 2.5 fusion.146
  60.2 4.1 convolution_convert_fusion.12
  65.0 54.6 %reduce-scatter.3.cloned.1.call-done = bf16[8,3072]{1,0:T(8,128)(2,1)} async-done(((bf16[128,3072]{1,0:T(8,128)(2,1)}), bf16[8,3072]{1,0:T(8,128)(2,1)}) %reduce-scatter.3.cloned.1.call-update) | async-done | bytes 49168 | tf_op jit(solution)/shard_map/while/body/eval_jaxpr/reduce_scatter | solution.py:44
  120.8 3.4 collective-permute-start
  124.2 3.2 collective-permute-done
  131.4 2.6 fusion.143
  134.4 39.9 %all_gather.33 = bf16[128,3072]{1,0:T(8,128)(2,1)S(1)} all-gather(bf16[8,3072]{1,0:T(8,128)(2,1)S(1)} %convolution_convert_fusion.11), channel_id=1, replica_groups=mesh['section'=2,'expert'=4,'dp'=4] {'expert','dp'}, dimensions={0}, use_global_device_ids=true | all-gather | bytes 835584 | tf_op jit(solution)/shard_map/while/body/eval_jaxpr/all_gather | solution.py:40
  175.2 2.5 fusion.146
  177.7 4.1 convolution_convert_fusion.12
  182.6 54.2 %reduce-scatter.3.cloned.1.call-done = bf16[8,3072]{1,0:T(8,128)(2,1)} async-done(((bf16[128,3072]{1,0:T(8,128)(2,1)}), bf16[8,3072]{1,0:T(8,128)(2,1)}) %reduce-scatter.3.cloned.1.call-update) | async-done | bytes 49168 | tf_op jit(solution)/shard_map/while/body/eval_jaxpr/reduce_scatter | solution.py:44
  238.0 3.4 collective-permute-start
  241.4 3.2 collective-permute-done
  248.5 2.6 fusion.143
  251.6 39.8 %all_gather.33 = bf16[128,3072]{1,0:T(8,128)(2,1)S(1)} all-gather(bf16[8,3072]{1,0:T(8,128)(2,1)S(1)} %convolution_convert_fusion.11), channel_id=1, replica_groups=mesh['section'=2,'expert'=4,'dp'=4] {'expert','dp'}, dimensions={0}, use_global_device_ids=true | all-gather | bytes 835584 | tf_op jit(solution)/shard_map/while/body/eval_jaxpr/all_gather | solution.py:40
  292.3 2.5 fusion.146
  294.8 4.1 convolution_convert_fusion.12
  299.6 54.2 %reduce-scatter.3.cloned.1.call-done = bf16[8,3072]{1,0:T(8,128)(2,1)} async-done(((bf16[128,3072]{1,0:T(8,128)(2,1)}), bf16[8,3072]{1,0:T(8,128)(2,1)}) %reduce-scatter.3.cloned.1.call-update) | async-done | bytes 49168 | tf_op jit(solution)/shard_map/while/body/eval_jaxpr/reduce_scatter | solution.py:44
  355.1 3.4 collective-permute-start
  358.5 3.2 collective-permute-done
  365.6 2.7 fusion.143
  368.7 40.0 %all_gather.33 = bf16[128,3072]{1,0:T(8,128)(2,1)S(1)} all-gather(bf16[8,3072]{1,0:T(8,128)(2,1)S(1)} %convolution_convert_fusion.11), channel_id=1, replica_groups=mesh['section'=2,'expert'=4,'dp'=4] {'expert','dp'}, dimensions={0}, use_global_device_ids=true | all-gather | bytes 835584 | tf_op jit(solution)/shard_map/while/body/eval_jaxpr/all_gather | solution.py:40
  409.6 2.5 fusion.146
  412.1 4.1 convolution_convert_fusion.12
  416.9 54.2 %reduce-scatter.3.cloned.1.call-done = bf16[8,3072]{1,0:T(8,128)(2,1)} async-done(((bf16[128,3072]{1,0:T(8,128)(2,1)}), bf16[8,3072]{1,0:T(8,128)(2,1)}) %reduce-scatter.3.cloned.1.call-update) | async-done | bytes 49168 | tf_op jit(solution)/shard_map/while/body/eval_jaxpr/reduce_scatter | solution.py:44
  472.3 3.4 collective-permute-start
  475.8 3.2 collective-permute-done
  482.9 2.7 fusion.143
  486.0 40.0 %all_gather.33 = bf16[128,3072]{1,0:T(8,128)(2,1)S(1)} all-gather(bf16[8,3072]{1,0:T(8,128)(2,1)S(1)} %convolution_convert_fusion.11), channel_id=1, replica_groups=mesh['section'=2,'expert'=4,'dp'=4] {'expert','dp'}, dimensions={0}, use_global_device_ids=true | all-gather | bytes 835584 | tf_op jit(solution)/shard_map/while/body/eval_jaxpr/all_gather | solution.py:40
  526.8 2.5 fusion.146
  529.3 4.1 convolution_convert_fusion.12
  534.2 54.2 %reduce-scatter.3.cloned.1.call-done = bf16[8,3072]{1,0:T(8,128)(2,1)} async-done(((bf16[128,3072]{1,0:T(8,128)(2,1)}), bf16[8,3072]{1,0:T(8,128)(2,1)}) %reduce-scatter.3.cloned.1.call-update) | async-done | bytes 49168 | tf_op jit(solution)/shard_map/while/body/eval_jaxpr/reduce_scatter | solution.py:44
  589.6 3.4 collective-permute-start
  593.0 3.2 collective-permute-done
  602.2 772.7 %while.43 = (s32[]{:T(128)}, bf16[32,3072]{1,0:T(8,128)(2,1)}, bf16[4,128,3072]{2,1,0:T(8,128)(2,1)}, bf16[4,128,3072]{2,1,0:T(8,128)(2,1)}, bf16[4,3,128,512]{3...) while((s32[]{:T(128)}, bf16[32,3072]{1,0:T(8,128)(2,1)}, ...), condition=%wide.region_13.14_spmd, body=%wide.region_6.13_spmd.sunk | while | flops 2025212544 | bytes 78193088 | solution.py:164
  607.5 40.1 %all_gather.34 = bf16[128,3072]{1,0:T(8,128)(2,1)S(1)} all-gather(bf16[8,3072]{1,0:T(8,128)(2,1)S(1)} %convolution_convert_fusion.13), channel_id=1, replica_groups=mesh['section'=2,'expert'=4,'dp'=4] {'expert','dp'}, dimensions={0}, use_global_device_ids=true | all-gather | bytes 835584 | tf_op jit(solution)/shard_map/while/body/eval_jaxpr/all_gather | solution.py:64
  649.1 35.2 %all_gather.35 = bf16[128,3072]{1,0:T(8,128)(2,1)S(1)} all-gather(bf16[8,3072]{1,0:T(8,128)(2,1)S(1)} %convolution_convert_fusion.14), channel_id=1, replica_groups=mesh['section'=2,'expert'=4,'dp'=4] {'expert','dp'}, dimensions={0}, use_global_device_ids=true | all-gather | bytes 835584 | tf_op jit(solution)/shard_map/while/body/eval_jaxpr/all_gather | solution.py:65
  696.4 51.1 %reduce-scatter.5.cloned.1.call-done = bf16[8,3072]{1,0:T(8,128)(2,1)} async-done(((bf16[128,3072]{1,0:T(8,128)(2,1)}), bf16[8,3072]{1,0:T(8,128)(2,1)}) %reduce-scatter.5.cloned.1.call-update) | async-done | bytes 49168 | tf_op jit(solution)/shard_map/while/body/eval_jaxpr/reduce_scatter | solution.py:79
  752.9 2.5 fusion.176
  755.4 2.4 collective-permute-done.1
  763.0 40.2 %all_gather.34 = bf16[128,3072]{1,0:T(8,128)(2,1)S(1)} all-gather(bf16[8,3072]{1,0:T(8,128)(2,1)S(1)} %convolution_convert_fusion.13), channel_id=1, replica_groups=mesh['section'=2,'expert'=4,'dp'=4] {'expert','dp'}, dimensions={0}, use_global_device_ids=true | all-gather | bytes 835584 | tf_op jit(solution)/shard_map/while/body/eval_jaxpr/all_gather | solution.py:64
  804.8 35.3 %all_gather.35 = bf16[128,3072]{1,0:T(8,128)(2,1)S(1)} all-gather(bf16[8,3072]{1,0:T(8,128)(2,1)S(1)} %convolution_convert_fusion.14), channel_id=1, replica_groups=mesh['section'=2,'expert'=4,'dp'=4] {'expert','dp'}, dimensions={0}, use_global_device_ids=true | all-gather | bytes 835584 | tf_op jit(solution)/shard_map/while/body/eval_jaxpr/all_gather | solution.py:65
  852.1 49.7 %reduce-scatter.5.cloned.1.call-done = bf16[8,3072]{1,0:T(8,128)(2,1)} async-done(((bf16[128,3072]{1,0:T(8,128)(2,1)}), bf16[8,3072]{1,0:T(8,128)(2,1)}) %reduce-scatter.5.cloned.1.call-update) | async-done | bytes 49168 | tf_op jit(solution)/shard_map/while/body/eval_jaxpr/reduce_scatter | solution.py:79
  907.2 2.5 fusion.176
  909.7 2.4 collective-permute-done.1
  917.3 39.7 %all_gather.34 = bf16[128,3072]{1,0:T(8,128)(2,1)S(1)} all-gather(bf16[8,3072]{1,0:T(8,128)(2,1)S(1)} %convolution_convert_fusion.13), channel_id=1, replica_groups=mesh['section'=2,'expert'=4,'dp'=4] {'expert','dp'}, dimensions={0}, use_global_device_ids=true | all-gather | bytes 835584 | tf_op jit(solution)/shard_map/while/body/eval_jaxpr/all_gather | solution.py:64
  958.6 35.3 %all_gather.35 = bf16[128,3072]{1,0:T(8,128)(2,1)S(1)} all-gather(bf16[8,3072]{1,0:T(8,128)(2,1)S(1)} %convolution_convert_fusion.14), channel_id=1, replica_groups=mesh['section'=2,'expert'=4,'dp'=4] {'expert','dp'}, dimensions={0}, use_global_device_ids=true | all-gather | bytes 835584 | tf_op jit(solution)/shard_map/while/body/eval_jaxpr/all_gather | solution.py:65
  1006.0 49.7 %reduce-scatter.5.cloned.1.call-done = bf16[8,3072]{1,0:T(8,128)(2,1)} async-done(((bf16[128,3072]{1,0:T(8,128)(2,1)}), bf16[8,3072]{1,0:T(8,128)(2,1)}) %reduce-scatter.5.cloned.1.call-update) | async-done | bytes 49168 | tf_op jit(solution)/shard_map/while/body/eval_jaxpr/reduce_scatter | solution.py:79
  1061.1 2.5 fusion.176
  1063.6 2.4 collective-permute-done.1
  1071.2 40.1 %all_gather.34 = bf16[128,3072]{1,0:T(8,128)(2,1)S(1)} all-gather(bf16[8,3072]{1,0:T(8,128)(2,1)S(1)} %convolution_convert_fusion.13), channel_id=1, replica_groups=mesh['section'=2,'expert'=4,'dp'=4] {'expert','dp'}, dimensions={0}, use_global_device_ids=true | all-gather | bytes 835584 | tf_op jit(solution)/shard_map/while/body/eval_jaxpr/all_gather | solution.py:64
  1112.9 35.3 %all_gather.35 = bf16[128,3072]{1,0:T(8,128)(2,1)S(1)} all-gather(bf16[8,3072]{1,0:T(8,128)(2,1)S(1)} %convolution_convert_fusion.14), channel_id=1, replica_groups=mesh['section'=2,'expert'=4,'dp'=4] {'expert','dp'}, dimensions={0}, use_global_device_ids=true | all-gather | bytes 835584 | tf_op jit(solution)/shard_map/while/body/eval_jaxpr/all_gather | solution.py:65
  1160.3 49.8 %reduce-scatter.5.cloned.1.call-done = bf16[8,3072]{1,0:T(8,128)(2,1)} async-done(((bf16[128,3072]{1,0:T(8,128)(2,1)}), bf16[8,3072]{1,0:T(8,128)(2,1)}) %reduce-scatter.5.cloned.1.call-update) | async-done | bytes 49168 | tf_op jit(solution)/shard_map/while/body/eval_jaxpr/reduce_scatter | solution.py:79
  1215.5 2.5 fusion.176
  1218.0 2.4 collective-permute-done.1
  1225.7 40.2 %all_gather.34 = bf16[128,3072]{1,0:T(8,128)(2,1)S(1)} all-gather(bf16[8,3072]{1,0:T(8,128)(2,1)S(1)} %convolution_convert_fusion.13), channel_id=1, replica_groups=mesh['section'=2,'expert'=4,'dp'=4] {'expert','dp'}, dimensions={0}, use_global_device_ids=true | all-gather | bytes 835584 | tf_op jit(solution)/shard_map/while/body/eval_jaxpr/all_gather | solution.py:64
  1267.5 35.3 %all_gather.35 = bf16[128,3072]{1,0:T(8,128)(2,1)S(1)} all-gather(bf16[8,3072]{1,0:T(8,128)(2,1)S(1)} %convolution_convert_fusion.14), channel_id=1, replica_groups=mesh['section'=2,'expert'=4,'dp'=4] {'expert','dp'}, dimensions={0}, use_global_device_ids=true | all-gather | bytes 835584 | tf_op jit(solution)/shard_map/while/body/eval_jaxpr/all_gather | solution.py:65
  1314.8 49.8 %reduce-scatter.5.cloned.1.call-done = bf16[8,3072]{1,0:T(8,128)(2,1)} async-done(((bf16[128,3072]{1,0:T(8,128)(2,1)}), bf16[8,3072]{1,0:T(8,128)(2,1)}) %reduce-scatter.5.cloned.1.call-update) | async-done | bytes 49168 | tf_op jit(solution)/shard_map/while/body/eval_jaxpr/reduce_scatter | solution.py:79
  1370.0 2.5 fusion.176
  1376.4 5.5 fusion.62
  1382.0 3.6 fusion.61
  1385.5 3.5 fusion.60
  (304 shorter events, 167.6 us)
Async XLA Ops:
  8.2 111.4 %reduce-scatter.3.cloned.1.call-start = ((), (), s32[]{:S(2)}) async-start(), calls=%async_computation.2 | async-start | bytes 835584 | tf_op jit(solution)/shard_map/while/body/eval_jaxpr/reduce_scatter | solution.py:44
  12.1 48.0 %copy-start = (bf16[3072,512]{1,0:T(8,128)(2,1)S(1)}, bf16[3072,512]{1,0:T(8,128)(2,1)}, u32[]{:S(2)}) copy-start(bf16[3072,512]{1,0:T(8,128)(2,1)} %get-tuple-element.941) | copy-start | bytes 9437188 | tf_op jit(solution)/shard_map/while
  14.8 42.0 %copy-start.9 = (bf16[32,3072]{1,0:T(8,128)(2,1)}, bf16[32,3072]{1,0:T(8,128)(2,1)S(1)}, u32[]{:S(2)}) copy-start(bf16[32,3072]{1,0:T(8,128)(2,1)S(1)} %get-tuple-element.873) | copy-start | bytes 589828 | tf_op jit(solution)/shard_map/while
  56.8 0.9 copy-start.8
  120.8 6.5 collective-permute-start
  127.4 109.4 %reduce-scatter.3.cloned.1.call-start = ((), (), s32[]{:S(2)}) async-start(), calls=%async_computation.2 | async-start | bytes 835584 | tf_op jit(solution)/shard_map/while/body/eval_jaxpr/reduce_scatter | solution.py:44
  131.3 46.4 %copy-start = (bf16[3072,512]{1,0:T(8,128)(2,1)S(1)}, bf16[3072,512]{1,0:T(8,128)(2,1)}, u32[]{:S(2)}) copy-start(bf16[3072,512]{1,0:T(8,128)(2,1)} %get-tuple-element.941) | copy-start | bytes 9437188 | tf_op jit(solution)/shard_map/while
  134.0 40.4 %copy-start.9 = (bf16[32,3072]{1,0:T(8,128)(2,1)}, bf16[32,3072]{1,0:T(8,128)(2,1)S(1)}, u32[]{:S(2)}) copy-start(bf16[32,3072]{1,0:T(8,128)(2,1)S(1)} %get-tuple-element.873) | copy-start | bytes 589828 | tf_op jit(solution)/shard_map/while
  238.0 6.6 collective-permute-start
  244.6 109.3 %reduce-scatter.3.cloned.1.call-start = ((), (), s32[]{:S(2)}) async-start(), calls=%async_computation.2 | async-start | bytes 835584 | tf_op jit(solution)/shard_map/while/body/eval_jaxpr/reduce_scatter | solution.py:44
  248.5 46.2 %copy-start = (bf16[3072,512]{1,0:T(8,128)(2,1)S(1)}, bf16[3072,512]{1,0:T(8,128)(2,1)}, u32[]{:S(2)}) copy-start(bf16[3072,512]{1,0:T(8,128)(2,1)} %get-tuple-element.941) | copy-start | bytes 9437188 | tf_op jit(solution)/shard_map/while
  251.2 40.2 %copy-start.9 = (bf16[32,3072]{1,0:T(8,128)(2,1)}, bf16[32,3072]{1,0:T(8,128)(2,1)S(1)}, u32[]{:S(2)}) copy-start(bf16[32,3072]{1,0:T(8,128)(2,1)S(1)} %get-tuple-element.873) | copy-start | bytes 589828 | tf_op jit(solution)/shard_map/while
  355.1 6.5 collective-permute-start
  361.6 109.5 %reduce-scatter.3.cloned.1.call-start = ((), (), s32[]{:S(2)}) async-start(), calls=%async_computation.2 | async-start | bytes 835584 | tf_op jit(solution)/shard_map/while/body/eval_jaxpr/reduce_scatter | solution.py:44
  365.6 46.5 %copy-start = (bf16[3072,512]{1,0:T(8,128)(2,1)S(1)}, bf16[3072,512]{1,0:T(8,128)(2,1)}, u32[]{:S(2)}) copy-start(bf16[3072,512]{1,0:T(8,128)(2,1)} %get-tuple-element.941) | copy-start | bytes 9437188 | tf_op jit(solution)/shard_map/while
  368.3 40.5 %copy-start.9 = (bf16[32,3072]{1,0:T(8,128)(2,1)}, bf16[32,3072]{1,0:T(8,128)(2,1)S(1)}, u32[]{:S(2)}) copy-start(bf16[32,3072]{1,0:T(8,128)(2,1)S(1)} %get-tuple-element.873) | copy-start | bytes 589828 | tf_op jit(solution)/shard_map/while
  472.3 6.6 collective-permute-start
  478.9 109.5 %reduce-scatter.3.cloned.1.call-start = ((), (), s32[]{:S(2)}) async-start(), calls=%async_computation.2 | async-start | bytes 835584 | tf_op jit(solution)/shard_map/while/body/eval_jaxpr/reduce_scatter | solution.py:44
  482.9 46.4 %copy-start = (bf16[3072,512]{1,0:T(8,128)(2,1)S(1)}, bf16[3072,512]{1,0:T(8,128)(2,1)}, u32[]{:S(2)}) copy-start(bf16[3072,512]{1,0:T(8,128)(2,1)} %get-tuple-element.941) | copy-start | bytes 9437188 | tf_op jit(solution)/shard_map/while
  485.6 40.4 %copy-start.9 = (bf16[32,3072]{1,0:T(8,128)(2,1)}, bf16[32,3072]{1,0:T(8,128)(2,1)S(1)}, u32[]{:S(2)}) copy-start(bf16[32,3072]{1,0:T(8,128)(2,1)S(1)} %get-tuple-element.873) | copy-start | bytes 589828 | tf_op jit(solution)/shard_map/while
  589.6 6.6 collective-permute-start
  598.1 4.1 copy-start.1
  598.1 4.1 copy-start.11
  602.2 145.3 %reduce-scatter.5.cloned.1.call-start = ((), (), s32[]{:S(2)}) async-start(), calls=%async_computation.3 | async-start | bytes 835584 | tf_op jit(solution)/shard_map/while/body/eval_jaxpr/reduce_scatter | solution.py:79
  607.4 77.5 %copy-start.3 = (bf16[512,3072]{1,0:T(8,128)(2,1)S(1)}, bf16[512,3072]{1,0:T(8,128)(2,1)}, u32[]{:S(2)}) copy-start(bf16[512,3072]{1,0:T(8,128)(2,1)} %get-tuple-element.1002) | copy-start | bytes 9437188 | tf_op jit(solution)/shard_map/while
  647.5 38.6 %copy-start.6 = (bf16[128,3072]{1,0:T(8,128)(2,1)}, bf16[128,3072]{1,0:T(8,128)(2,1)S(1)}, u32[]{:S(2)}) copy-start(bf16[128,3072]{1,0:T(8,128)(2,1)S(1)} %all_gather.34) | copy-start | bytes 2359300 | tf_op jit(solution)/shard_map/while
  684.4 1.8 copy-start.4
  684.9 1.9 copy-start.2
  690.8 2.3 copy-start.7
  690.8 4.0 copy-start.5
  750.1 7.7 collective-permute-start.1
  757.8 144.0 %reduce-scatter.5.cloned.1.call-start = ((), (), s32[]{:S(2)}) async-start(), calls=%async_computation.3 | async-start | bytes 835584 | tf_op jit(solution)/shard_map/while/body/eval_jaxpr/reduce_scatter | solution.py:79
  763.0 77.6 %copy-start.3 = (bf16[512,3072]{1,0:T(8,128)(2,1)S(1)}, bf16[512,3072]{1,0:T(8,128)(2,1)}, u32[]{:S(2)}) copy-start(bf16[512,3072]{1,0:T(8,128)(2,1)} %get-tuple-element.1002) | copy-start | bytes 9437188 | tf_op jit(solution)/shard_map/while
  803.2 38.6 %copy-start.6 = (bf16[128,3072]{1,0:T(8,128)(2,1)}, bf16[128,3072]{1,0:T(8,128)(2,1)S(1)}, u32[]{:S(2)}) copy-start(bf16[128,3072]{1,0:T(8,128)(2,1)S(1)} %all_gather.34) | copy-start | bytes 2359300 | tf_op jit(solution)/shard_map/while
  840.0 1.8 copy-start.4
  840.6 1.9 copy-start.2
  846.4 2.3 copy-start.7
  846.4 4.0 copy-start.5
  904.4 7.7 collective-permute-start.1
  912.1 143.6 %reduce-scatter.5.cloned.1.call-start = ((), (), s32[]{:S(2)}) async-start(), calls=%async_computation.3 | async-start | bytes 835584 | tf_op jit(solution)/shard_map/while/body/eval_jaxpr/reduce_scatter | solution.py:79
  917.3 77.2 %copy-start.3 = (bf16[512,3072]{1,0:T(8,128)(2,1)S(1)}, bf16[512,3072]{1,0:T(8,128)(2,1)}, u32[]{:S(2)}) copy-start(bf16[512,3072]{1,0:T(8,128)(2,1)} %get-tuple-element.1002) | copy-start | bytes 9437188 | tf_op jit(solution)/shard_map/while
  957.0 38.7 %copy-start.6 = (bf16[128,3072]{1,0:T(8,128)(2,1)}, bf16[128,3072]{1,0:T(8,128)(2,1)S(1)}, u32[]{:S(2)}) copy-start(bf16[128,3072]{1,0:T(8,128)(2,1)S(1)} %all_gather.34) | copy-start | bytes 2359300 | tf_op jit(solution)/shard_map/while
  993.9 1.8 copy-start.4
  994.5 1.9 copy-start.2
  1000.3 2.3 copy-start.7
  1000.3 4.0 copy-start.5
  1058.4 7.7 collective-permute-start.1
  1066.0 144.1 %reduce-scatter.5.cloned.1.call-start = ((), (), s32[]{:S(2)}) async-start(), calls=%async_computation.3 | async-start | bytes 835584 | tf_op jit(solution)/shard_map/while/body/eval_jaxpr/reduce_scatter | solution.py:79
  1071.2 77.6 %copy-start.3 = (bf16[512,3072]{1,0:T(8,128)(2,1)S(1)}, bf16[512,3072]{1,0:T(8,128)(2,1)}, u32[]{:S(2)}) copy-start(bf16[512,3072]{1,0:T(8,128)(2,1)} %get-tuple-element.1002) | copy-start | bytes 9437188 | tf_op jit(solution)/shard_map/while
  1111.3 38.7 %copy-start.6 = (bf16[128,3072]{1,0:T(8,128)(2,1)}, bf16[128,3072]{1,0:T(8,128)(2,1)S(1)}, u32[]{:S(2)}) copy-start(bf16[128,3072]{1,0:T(8,128)(2,1)S(1)} %all_gather.34) | copy-start | bytes 2359300 | tf_op jit(solution)/shard_map/while
  1148.2 1.8 copy-start.4
  1148.8 1.9 copy-start.2
  1154.6 2.3 copy-start.7
  1154.6 4.0 copy-start.5
  1212.8 7.7 collective-permute-start.1
  1220.5 144.2 %reduce-scatter.5.cloned.1.call-start = ((), (), s32[]{:S(2)}) async-start(), calls=%async_computation.3 | async-start | bytes 835584 | tf_op jit(solution)/shard_map/while/body/eval_jaxpr/reduce_scatter | solution.py:79
  1225.7 77.7 %copy-start.3 = (bf16[512,3072]{1,0:T(8,128)(2,1)S(1)}, bf16[512,3072]{1,0:T(8,128)(2,1)}, u32[]{:S(2)}) copy-start(bf16[512,3072]{1,0:T(8,128)(2,1)} %get-tuple-element.1002) | copy-start | bytes 9437188 | tf_op jit(solution)/shard_map/while
  1265.9 38.7 %copy-start.6 = (bf16[128,3072]{1,0:T(8,128)(2,1)}, bf16[128,3072]{1,0:T(8,128)(2,1)S(1)}, u32[]{:S(2)}) copy-start(bf16[128,3072]{1,0:T(8,128)(2,1)S(1)} %all_gather.34) | copy-start | bytes 2359300 | tf_op jit(solution)/shard_map/while
  1302.7 1.8 copy-start.4
  1303.3 1.9 copy-start.2
  1309.1 2.3 copy-start.7
  1309.2 4.0 copy-start.5
  1367.3 7.7 collective-permute-start.1
  1376.4 5.6 copy-start.10
  (4 other events, 3.5 us)
Sparse Core Ops, SparseCore 0:
  64.5 55.1 reduce-scatter.2
  182.0 54.7 reduce-scatter.2
  299.1 54.7 reduce-scatter.2
  416.4 54.7 reduce-scatter.2
  533.6 54.7 reduce-scatter.2
  690.9 56.5 reduce-scatter.4
  846.5 55.2 reduce-scatter.4
  1000.4 55.2 reduce-scatter.4
  1154.8 55.3 reduce-scatter.4
  1309.3 55.3 reduce-scatter.4
where the time goes:
time: 1400 us
  blocking collectives  578 us (41%)
  waiting for transfers between devices  550 us (39%)
  matrix products  102 us (7%)
  other arithmetic  84.4 us (6%)
  local copies, waits for them, and re-layouts  43.7 us (3%)
  starting transfers between devices  23.4 us (2%)
  between operations  14 us (1%)
    reduce_scatter x5, waiting for transfers between devices, layer_forward(): lax.psum_scatter(jnp.dot(hidden, down_w, preferred_element_type=jnp.float...  271 us
    reduce_scatter x5, waiting for transfers between devices, layer_backward(): lax.psum_scatter((lax.dot_general(gate_pre_grad, gate_w, contract_rows, p...  250 us
    all_gather x5, blocking collectives, layer_forward(): rows = lax.all_gather(send_rows, ('expert', 'dp'), axis=0, tiled=True)  201 us
    all_gather x5, blocking collectives, layer_backward(): lax.all_gather(send_rows, ('expert', 'dp'), axis=0, tiled=True)  200 us
    all_gather x5, blocking collectives, layer_backward(): lax.all_gather(send_grad, ('expert', 'dp'), axis=0, tiled=True)  176 us
    scatter x20, other arithmetic, store_if(): return store.at[index].set(jnp.where(valid, value, older))  42.4 us
  transfers between devices with their start and end apart: 20, of which 20 were waited for; matrix products, arithmetic and copies ran while one was open for 4% of the time, Pallas kernels for 0%

commit v1 on v0

--- a/solution.py
+++ b/solution.py
@@ -37,7 +37,30 @@
     input_f, scale, normed = normalize(layer_input)
     table = slot_table(mask_row)
     send_rows = pick_rows(table, normed)
-    rows = lax.all_gather(send_rows, ("expert", "dp"), axis=0, tiled=True)
+    length, place, extent = (
+        lax.axis_size(("expert", "dp")),
+        lax.axis_index(("expert", "dp")),
+        send_rows.shape[0],
+    )
+    right = [(i_2, (i_2 + 1) % length) for i_2 in range(length)]
+    left = [(i_2, (i_2 - 1) % length) for i_2 in range(length)]
+    whole = jnp.zeros(
+        (*send_rows.shape[:0], length * extent, *send_rows.shape[0 + 1 :]), send_rows.dtype
+    )
+    whole = lax.dynamic_update_slice_in_dim(whole, send_rows, place * extent, axis=0)
+    from_left = from_right = send_rows
+    half = length // 2
+    for lap in range(1, half + 1):
+        from_left = lax.ppermute(from_left, ("expert", "dp"), right)
+        whole = lax.dynamic_update_slice_in_dim(
+            whole, from_left, (place - lap) % length * extent, axis=0
+        )
+        if lap < length - half:
+            from_right = lax.ppermute(from_right, ("expert", "dp"), left)
+            whole = lax.dynamic_update_slice_in_dim(
+                whole, from_right, (place + lap) % length * extent, axis=0
+            )
+    rows = whole
     gate_pre = jnp.dot(rows, gate_w, preferred_element_type=jnp.float32)
     up_pre = jnp.dot(rows, up_w, preferred_element_type=jnp.float32)
     hidden = (jax.nn.silu(gate_pre) * up_pre).astype(jnp.bfloat16)

time: 1400 us -> 1460 us (1.043)
  blocking collectives: 578 us -> 377 us
  starting transfers between devices: 23.4 us -> 162 us
  waiting for transfers between devices: 550 us -> 632 us
  local copies, waits for them, and re-layouts: 43.7 us -> 87.6 us
    all_gather x5 -> x0, blocking collectives: 201 us -> none  [layer_forward(): rows = lax.all_gather(send_rows, ('expert', 'dp'), axis=0, tiled=True)]
    ppermute x0 -> x75, starting transfers between devices: none -> 139 us  [the longest x35 129 us: layer_forward(): from_right = lax.ppermute(from_right, ('expert', 'dp'), left)]
    ppermute x0 -> x75, waiting for transfers between devices: none -> 79.1 us  [the longest x40 58.4 us: layer_forward(): from_left = lax.ppermute(from_left, ('expert', 'dp'), right)]
    dynamic_update_slice x0 -> x75, local copies, waits for them, and re-layouts: none -> 46.7 us  [the longest x40 24.9 us: layer_forward(): lax.dynamic_update_slice_in_dim(whole, from_left, (place - lap) % length...]
  transfers between devices with their start and end apart: 20 -> 95, of which waited for: 20 -> 74; matrix products, arithmetic and copies ran while one was open for 4% -> 6% of each run, Pallas kernels for 0% -> 0%
where the time goes in v1:
time: 1460 us
  waiting for transfers between devices  632 us (43%)
  blocking collectives  377 us (26%)
  starting transfers between devices  162 us (11%)
  matrix products  113 us (8%)
  local copies, waits for them, and re-layouts  87.6 us (6%)
  other arithmetic  74.2 us (5%)
    reduce_scatter x5, waiting for transfers between devices, layer_forward(): lax.psum_scatter(jnp.dot(hidden, down_w, preferred_element_type=jnp.float...  273 us
    reduce_scatter x5, waiting for transfers between devices, layer_backward(): lax.psum_scatter((lax.dot_general(gate_pre_grad, gate_w, contract_rows, p...  249 us
    all_gather x5, blocking collectives, layer_backward(): lax.all_gather(send_rows, ('expert', 'dp'), axis=0, tiled=True)  200 us
    all_gather x5, blocking collectives, layer_backward(): lax.all_gather(send_grad, ('expert', 'dp'), axis=0, tiled=True)  177 us
    ppermute x35, starting transfers between devices, layer_forward(): from_right = lax.ppermute(from_right, ('expert', 'dp'), left)  129 us
    ppermute x40, waiting for transfers between devices, layer_forward(): from_left = lax.ppermute(from_left, ('expert', 'dp'), right)  58.4 us
    scatter x20, other arithmetic, store_if(): return store.at[index].set(jnp.where(valid, value, older))  41.6 us
    ppermute x10, waiting for transfers between devices, shifted(): return lax.ppermute(block, axis, route)  31.2 us
  transfers between devices with their start and end apart: 95, of which 74 were waited for; matrix products, arithmetic and copies ran while one was open for 6% of the time, Pallas kernels for 0%

profile of v1, /device:TPU:0, one launch (start us, length us, event | category | flops | bytes accessed | tf_op | source)
XLA Modules:
  0.0 1460.9 jit_solution(14714098769517229894)
XLA Ops:
  8.2 659.4 %while.43 = (s32[]{:T(128)}, bf16[32,3072]{1,0:T(8,128)(2,1)S(1)}, bf16[4,32,3072]{2,1,0:T(8,128)(2,1)}, s32[]{:T(128)}, pred[]{:T(512)}, /*index=5*/bf16[4,32,3...) while((s32[]{:T(128)}, bf16[32,3072]{1,0:T(8,128)(2,1)S(1)}, ...), condition=%wide.region_5.6_spmd, body=%wide.region_0.5_spmd.sunk | while | flops 1213294976 | bytes 35724864 | solution.py:160
  16.5 5.4 collective-permute-start.1
  23.7 4.5 collective-permute-start.3
  30.0 4.4 collective-permute-start.5
  36.3 4.4 collective-permute-start.7
  42.9 4.4 collective-permute-start.9
  49.1 4.6 collective-permute-start.11
  55.9 4.8 collective-permute-start.13
  61.9 5.3 collective-permute-done.12
  68.4 5.0 collective-permute-done.14
  77.4 4.2 convolution_convert_fusion.10
  82.4 53.3 %reduce-scatter.3.cloned.1.call-done = bf16[8,3072]{1,0:T(8,128)(2,1)} async-done(((bf16[128,3072]{1,0:T(8,128)(2,1)}), bf16[8,3072]{1,0:T(8,128)(2,1)}) %reduce-scatter.3.cloned.1.call-update) | async-done | bytes 49168 | tf_op jit(solution)/shard_map/while/body/eval_jaxpr/reduce_scatter | solution.py:67
  160.2 3.9 collective-permute-start.5
  166.2 4.6 collective-permute-start.7
  172.8 4.6 collective-permute-start.9
  179.1 4.5 collective-permute-start.11
  185.4 4.5 collective-permute-start.13
  191.6 5.0 collective-permute-done.12
  197.8 5.0 collective-permute-done.14
  206.9 4.2 convolution_convert_fusion.10
  211.8 54.9 %reduce-scatter.3.cloned.1.call-done = bf16[8,3072]{1,0:T(8,128)(2,1)} async-done(((bf16[128,3072]{1,0:T(8,128)(2,1)}), bf16[8,3072]{1,0:T(8,128)(2,1)}) %reduce-scatter.3.cloned.1.call-update) | async-done | bytes 49168 | tf_op jit(solution)/shard_map/while/body/eval_jaxpr/reduce_scatter | solution.py:67
  291.3 4.0 collective-permute-start.5
  297.3 4.6 collective-permute-start.7
  303.8 4.6 collective-permute-start.9
  310.1 4.5 collective-permute-start.11
  316.4 4.4 collective-permute-start.13
  322.7 5.0 collective-permute-done.12
  328.9 5.0 collective-permute-done.14
  337.9 4.2 convolution_convert_fusion.10
  342.9 54.9 %reduce-scatter.3.cloned.1.call-done = bf16[8,3072]{1,0:T(8,128)(2,1)} async-done(((bf16[128,3072]{1,0:T(8,128)(2,1)}), bf16[8,3072]{1,0:T(8,128)(2,1)}) %reduce-scatter.3.cloned.1.call-update) | async-done | bytes 49168 | tf_op jit(solution)/shard_map/while/body/eval_jaxpr/reduce_scatter | solution.py:67
  422.3 4.0 collective-permute-start.5
  428.4 4.6 collective-permute-start.7
  434.9 4.6 collective-permute-start.9
  441.2 4.5 collective-permute-start.11
  447.4 4.5 collective-permute-start.13
  453.7 5.0 collective-permute-done.12
  459.9 5.0 collective-permute-done.14
  468.9 4.2 convolution_convert_fusion.10
  473.8 55.0 %reduce-scatter.3.cloned.1.call-done = bf16[8,3072]{1,0:T(8,128)(2,1)} async-done(((bf16[128,3072]{1,0:T(8,128)(2,1)}), bf16[8,3072]{1,0:T(8,128)(2,1)}) %reduce-scatter.3.cloned.1.call-update) | async-done | bytes 49168 | tf_op jit(solution)/shard_map/while/body/eval_jaxpr/reduce_scatter | solution.py:67
  559.3 4.6 collective-permute-start.7
  566.0 4.6 collective-permute-start.9
  572.3 4.5 collective-permute-start.11
  578.6 4.4 collective-permute-start.13
  584.9 5.0 collective-permute-done.12
  591.1 5.0 collective-permute-done.14
  600.1 4.2 convolution_convert_fusion.10
  605.1 54.8 %reduce-scatter.3.cloned.1.call-done = bf16[8,3072]{1,0:T(8,128)(2,1)} async-done(((bf16[128,3072]{1,0:T(8,128)(2,1)}), bf16[8,3072]{1,0:T(8,128)(2,1)}) %reduce-scatter.3.cloned.1.call-update) | async-done | bytes 49168 | tf_op jit(solution)/shard_map/while/body/eval_jaxpr/reduce_scatter | solution.py:67
  673.6 766.3 %while.44 = (s32[]{:T(128)}, bf16[32,3072]{1,0:T(8,128)(2,1)}, bf16[4,128,3072]{2,1,0:T(8,128)(2,1)}, bf16[4,128,3072]{2,1,0:T(8,128)(2,1)}, bf16[4,3,128,512]{3...) while((s32[]{:T(128)}, bf16[32,3072]{1,0:T(8,128)(2,1)}, ...), condition=%wide.region_13.14_spmd, body=%wide.region_6.13_spmd.sunk | while | flops 2025212544 | bytes 78193088 | solution.py:187
  677.0 40.1 %all_gather.22 = bf16[128,3072]{1,0:T(8,128)(2,1)S(1)} all-gather(bf16[8,3072]{1,0:T(8,128)(2,1)S(1)} %convolution_convert_fusion.11), channel_id=1, replica_groups=mesh['section'=2,'expert'=4,'dp'=4] {'expert','dp'}, dimensions={0}, use_global_device_ids=true | all-gather | bytes 835584 | tf_op jit(solution)/shard_map/while/body/eval_jaxpr/all_gather | solution.py:87
  718.7 35.1 %all_gather.23 = bf16[128,3072]{1,0:T(8,128)(2,1)S(1)} all-gather(bf16[8,3072]{1,0:T(8,128)(2,1)S(1)} %convolution_convert_fusion.12), channel_id=1, replica_groups=mesh['section'=2,'expert'=4,'dp'=4] {'expert','dp'}, dimensions={0}, use_global_device_ids=true | all-gather | bytes 835584 | tf_op jit(solution)/shard_map/while/body/eval_jaxpr/all_gather | solution.py:88
  766.7 51.2 %reduce-scatter.5.cloned.1.call-done = bf16[8,3072]{1,0:T(8,128)(2,1)} async-done(((bf16[128,3072]{1,0:T(8,128)(2,1)}), bf16[8,3072]{1,0:T(8,128)(2,1)}) %reduce-scatter.5.cloned.1.call-update) | async-done | bytes 49168 | tf_op jit(solution)/shard_map/while/body/eval_jaxpr/reduce_scatter | solution.py:102
  831.5 40.2 %all_gather.22 = bf16[128,3072]{1,0:T(8,128)(2,1)S(1)} all-gather(bf16[8,3072]{1,0:T(8,128)(2,1)S(1)} %convolution_convert_fusion.11), channel_id=1, replica_groups=mesh['section'=2,'expert'=4,'dp'=4] {'expert','dp'}, dimensions={0}, use_global_device_ids=true | all-gather | bytes 835584 | tf_op jit(solution)/shard_map/while/body/eval_jaxpr/all_gather | solution.py:87
  873.3 35.4 %all_gather.23 = bf16[128,3072]{1,0:T(8,128)(2,1)S(1)} all-gather(bf16[8,3072]{1,0:T(8,128)(2,1)S(1)} %convolution_convert_fusion.12), channel_id=1, replica_groups=mesh['section'=2,'expert'=4,'dp'=4] {'expert','dp'}, dimensions={0}, use_global_device_ids=true | all-gather | bytes 835584 | tf_op jit(solution)/shard_map/while/body/eval_jaxpr/all_gather | solution.py:88
  921.6 49.4 %reduce-scatter.5.cloned.1.call-done = bf16[8,3072]{1,0:T(8,128)(2,1)} async-done(((bf16[128,3072]{1,0:T(8,128)(2,1)}), bf16[8,3072]{1,0:T(8,128)(2,1)}) %reduce-scatter.5.cloned.1.call-update) | async-done | bytes 49168 | tf_op jit(solution)/shard_map/while/body/eval_jaxpr/reduce_scatter | solution.py:102
  984.6 40.0 %all_gather.22 = bf16[128,3072]{1,0:T(8,128)(2,1)S(1)} all-gather(bf16[8,3072]{1,0:T(8,128)(2,1)S(1)} %convolution_convert_fusion.11), channel_id=1, replica_groups=mesh['section'=2,'expert'=4,'dp'=4] {'expert','dp'}, dimensions={0}, use_global_device_ids=true | all-gather | bytes 835584 | tf_op jit(solution)/shard_map/while/body/eval_jaxpr/all_gather | solution.py:87
  1026.2 35.4 %all_gather.23 = bf16[128,3072]{1,0:T(8,128)(2,1)S(1)} all-gather(bf16[8,3072]{1,0:T(8,128)(2,1)S(1)} %convolution_convert_fusion.12), channel_id=1, replica_groups=mesh['section'=2,'expert'=4,'dp'=4] {'expert','dp'}, dimensions={0}, use_global_device_ids=true | all-gather | bytes 835584 | tf_op jit(solution)/shard_map/while/body/eval_jaxpr/all_gather | solution.py:88
  1074.5 49.3 %reduce-scatter.5.cloned.1.call-done = bf16[8,3072]{1,0:T(8,128)(2,1)} async-done(((bf16[128,3072]{1,0:T(8,128)(2,1)}), bf16[8,3072]{1,0:T(8,128)(2,1)}) %reduce-scatter.5.cloned.1.call-update) | async-done | bytes 49168 | tf_op jit(solution)/shard_map/while/body/eval_jaxpr/reduce_scatter | solution.py:102
  1137.4 39.8 %all_gather.22 = bf16[128,3072]{1,0:T(8,128)(2,1)S(1)} all-gather(bf16[8,3072]{1,0:T(8,128)(2,1)S(1)} %convolution_convert_fusion.11), channel_id=1, replica_groups=mesh['section'=2,'expert'=4,'dp'=4] {'expert','dp'}, dimensions={0}, use_global_device_ids=true | all-gather | bytes 835584 | tf_op jit(solution)/shard_map/while/body/eval_jaxpr/all_gather | solution.py:87
  1178.8 35.3 %all_gather.23 = bf16[128,3072]{1,0:T(8,128)(2,1)S(1)} all-gather(bf16[8,3072]{1,0:T(8,128)(2,1)S(1)} %convolution_convert_fusion.12), channel_id=1, replica_groups=mesh['section'=2,'expert'=4,'dp'=4] {'expert','dp'}, dimensions={0}, use_global_device_ids=true | all-gather | bytes 835584 | tf_op jit(solution)/shard_map/while/body/eval_jaxpr/all_gather | solution.py:88
  1227.0 49.6 %reduce-scatter.5.cloned.1.call-done = bf16[8,3072]{1,0:T(8,128)(2,1)} async-done(((bf16[128,3072]{1,0:T(8,128)(2,1)}), bf16[8,3072]{1,0:T(8,128)(2,1)}) %reduce-scatter.5.cloned.1.call-update) | async-done | bytes 49168 | tf_op jit(solution)/shard_map/while/body/eval_jaxpr/reduce_scatter | solution.py:102
  1290.3 40.1 %all_gather.22 = bf16[128,3072]{1,0:T(8,128)(2,1)S(1)} all-gather(bf16[8,3072]{1,0:T(8,128)(2,1)S(1)} %convolution_convert_fusion.11), channel_id=1, replica_groups=mesh['section'=2,'expert'=4,'dp'=4] {'expert','dp'}, dimensions={0}, use_global_device_ids=true | all-gather | bytes 835584 | tf_op jit(solution)/shard_map/while/body/eval_jaxpr/all_gather | solution.py:87
  1331.9 35.4 %all_gather.23 = bf16[128,3072]{1,0:T(8,128)(2,1)S(1)} all-gather(bf16[8,3072]{1,0:T(8,128)(2,1)S(1)} %convolution_convert_fusion.12), channel_id=1, replica_groups=mesh['section'=2,'expert'=4,'dp'=4] {'expert','dp'}, dimensions={0}, use_global_device_ids=true | all-gather | bytes 835584 | tf_op jit(solution)/shard_map/while/body/eval_jaxpr/all_gather | solution.py:88
  1380.2 49.4 %reduce-scatter.5.cloned.1.call-done = bf16[8,3072]{1,0:T(8,128)(2,1)} async-done(((bf16[128,3072]{1,0:T(8,128)(2,1)}), bf16[8,3072]{1,0:T(8,128)(2,1)}) %reduce-scatter.5.cloned.1.call-update) | async-done | bytes 49168 | tf_op jit(solution)/shard_map/while/body/eval_jaxpr/reduce_scatter | solution.py:102
  1441.4 5.5 fusion.56
  (513 shorter events, 353.4 us)
Async XLA Ops:
  8.2 127.5 %reduce-scatter.3.cloned.1.call-start = ((), (), s32[]{:S(2)}) async-start(), calls=%async_computation.2 | async-start | bytes 835584 | tf_op jit(solution)/shard_map/while/body/eval_jaxpr/reduce_scatter | solution.py:67
  16.5 7.2 collective-permute-start.1
  21.9 6.9 collective-permute-start
  23.7 6.4 collective-permute-start.3
  28.8 6.3 collective-permute-start.2
  30.0 6.3 collective-permute-start.5
  35.1 6.6 collective-permute-start.4
  36.3 6.6 collective-permute-start.7
  49.1 6.7 collective-permute-start.11
  54.1 6.5 collective-permute-start.10
  55.9 11.9 collective-permute-start.13
  60.6 6.6 collective-permute-start.12
  136.7 6.6 collective-permute-start.15
  143.3 123.5 %reduce-scatter.3.cloned.1.call-start = ((), (), s32[]{:S(2)}) async-start(), calls=%async_computation.2 | async-start | bytes 835584 | tf_op jit(solution)/shard_map/while/body/eval_jaxpr/reduce_scatter | solution.py:67
  151.6 6.4 collective-permute-start
  158.0 6.3 collective-permute-start.2
  164.3 6.5 collective-permute-start.4
  166.2 6.6 collective-permute-start.7
  170.8 6.6 collective-permute-start.6
  172.8 6.3 collective-permute-start.9
  177.4 6.7 collective-permute-start.8
  184.1 6.3 collective-permute-start.10
  185.4 11.9 collective-permute-start.13
  267.8 6.6 collective-permute-start.15
  274.4 123.4 %reduce-scatter.3.cloned.1.call-start = ((), (), s32[]{:S(2)}) async-start(), calls=%async_computation.2 | async-start | bytes 835584 | tf_op jit(solution)/shard_map/while/body/eval_jaxpr/reduce_scatter | solution.py:67
  282.7 6.4 collective-permute-start
  295.3 6.6 collective-permute-start.4
  297.3 6.5 collective-permute-start.7
  301.9 6.5 collective-permute-start.6
  303.8 6.4 collective-permute-start.9
  308.4 6.7 collective-permute-start.8
  315.1 6.3 collective-permute-start.10
  316.4 11.9 collective-permute-start.13
  398.9 6.6 collective-permute-start.15
  405.4 123.4 %reduce-scatter.3.cloned.1.call-start = ((), (), s32[]{:S(2)}) async-start(), calls=%async_computation.2 | async-start | bytes 835584 | tf_op jit(solution)/shard_map/while/body/eval_jaxpr/reduce_scatter | solution.py:67
  413.8 6.3 collective-permute-start
  426.4 6.6 collective-permute-start.4
  428.4 6.5 collective-permute-start.7
  433.0 6.5 collective-permute-start.6
  434.9 6.4 collective-permute-start.9
  439.5 6.7 collective-permute-start.8
  446.2 6.3 collective-permute-start.10
  447.4 11.8 collective-permute-start.13
  529.9 6.6 collective-permute-start.15
  536.5 123.4 %reduce-scatter.3.cloned.1.call-start = ((), (), s32[]{:S(2)}) async-start(), calls=%async_computation.2 | async-start | bytes 835584 | tf_op jit(solution)/shard_map/while/body/eval_jaxpr/reduce_scatter | solution.py:67
  544.8 6.4 collective-permute-start
  557.5 6.5 collective-permute-start.4
  559.3 6.7 collective-permute-start.7
  564.0 6.6 collective-permute-start.6
  566.0 6.4 collective-permute-start.9
  570.6 6.8 collective-permute-start.8
  577.3 6.3 collective-permute-start.10
  578.6 11.9 collective-permute-start.13
  661.0 6.6 collective-permute-start.15
  673.6 144.3 %reduce-scatter.5.cloned.1.call-start = ((), (), s32[]{:S(2)}) async-start(), calls=%async_computation.3 | async-start | bytes 835584 | tf_op jit(solution)/shard_map/while/body/eval_jaxpr/reduce_scatter | solution.py:102
  820.6 7.7 collective-permute-start.16
  828.3 142.8 %reduce-scatter.5.cloned.1.call-start = ((), (), s32[]{:S(2)}) async-start(), calls=%async_computation.3 | async-start | bytes 835584 | tf_op jit(solution)/shard_map/while/body/eval_jaxpr/reduce_scatter | solution.py:102
  973.7 7.7 collective-permute-start.16
  981.3 142.5 %reduce-scatter.5.cloned.1.call-start = ((), (), s32[]{:S(2)}) async-start(), calls=%async_computation.3 | async-start | bytes 835584 | tf_op jit(solution)/shard_map/while/body/eval_jaxpr/reduce_scatter | solution.py:102
  1126.5 7.7 collective-permute-start.16
  1134.1 142.5 %reduce-scatter.5.cloned.1.call-start = ((), (), s32[]{:S(2)}) async-start(), calls=%async_computation.3 | async-start | bytes 835584 | tf_op jit(solution)/shard_map/while/body/eval_jaxpr/reduce_scatter | solution.py:102
  1279.3 7.7 collective-permute-start.16
  1287.0 142.7 %reduce-scatter.5.cloned.1.call-start = ((), (), s32[]{:S(2)}) async-start(), calls=%async_computation.3 | async-start | bytes 835584 | tf_op jit(solution)/shard_map/while/body/eval_jaxpr/reduce_scatter | solution.py:102
  1432.3 7.7 collective-permute-start.16
  (71 other events, 1112.7 us)
Sparse Core Ops, SparseCore 0:
  81.8 53.7 reduce-scatter.2
  211.2 55.4 reduce-scatter.2
  342.3 55.4 reduce-scatter.2
  473.3 55.5 reduce-scatter.2
  604.5 55.3 reduce-scatter.2
  761.0 56.9 reduce-scatter.4
  915.9 55.1 reduce-scatter.4
  1068.7 55.0 reduce-scatter.4
  1221.3 55.3 reduce-scatter.4
  1374.5 55.0 reduce-scatter.4
